TPU v7x, 32 devices: a whole 2x2x4 slice. The times are simulated.
32 devices in a mesh: tile: 8 (over z, y), rec: 4 (over x, core).
Axes of the slice: x: 2, y: 2, z: 4, core: 2. Of those that a mesh axis runs over, the one named last changes fastest.
Arguments:
- screens: bfloat16 [2, 384, 128, 128], P(None, 'tile', 'rec'), may hold values from -1.796875 to 1.796875
- tile_owner: int32 [2, 2, 1024, 1], replicated, may hold values from 0 to 7; in each aligned block of 128 rows (0 to 127, 128 to 255, ..., all dimensions but the last counted through in order) at most 24 rows name the same one
- tile_slot: int32 [2, 2, 1024], replicated, may hold values from 0 to 47
- commands_init: float32 [4096], P('rec'), may hold values from -1.2 to 1.2
- reconstructor: bfloat16 [32, 16, 128, 128], P('rec', 'tile'), may hold values from -1 to 1
- pattern: int32 [32, 16], P('rec', 'tile'), may hold values from 0 to 31
Outputs:
- lgs_slopes: float32 [2, 32, 128], P(None, 'tile', 'rec')
- science_residual: bfloat16 [2, 992, 128, 128], P(None, 'tile', 'rec')
- commands: float32 [4096], P('rec')
Inputs may be any that keep to these rules, and one draw needn't show every extreme that they name: `tile_owner`: within the 128 consecutive entries of one index of tile for one frame and layer, each holder is named at most 24 times; in every frame and layer some such entries name one holder exactly 24 times.
All inputs are finite; a program needn't handle non-finite values.
Results may differ from a plain program's by a relative error of at most 0.011.
Values may be sent and summed in bfloat16 or wider, within the bound.
No kernel may reach another device: no remote copies, remote signals or barrier semaphores. Data moves between devices by JAX's collectives and lax.ppermute only.
A program may use at most 64 MiB of HBM per device.

v0:
```python
import math
import jax
import jax.numpy as jnp
from jax import lax
from jax.sharding import PartitionSpec as P

SUBPX = 16
SPOT = 32
SUB = 8
PT = 64
LG_DEV = 4
SC_DEV = 124
loop_gain = 0.5


def influence(tile_px, sub_px, sub_count):
    pixel = jnp.arange(tile_px, dtype=jnp.float32)[:, None] + 0.5
    centre = (jnp.arange(sub_count, dtype=jnp.float32)[None, :] + 0.5) * sub_px
    return jnp.maximum(0.0, 1.0 - jnp.abs(pixel - centre) / sub_px)


def tables(spot_px, sub_px):
    freq = jnp.arange(spot_px, dtype=jnp.int32)[:, None]
    pixel = jnp.arange(sub_px, dtype=jnp.int32)[None, :]
    turns = (freq * pixel % spot_px).astype(jnp.float32) * (2.0 * math.pi / spot_px)
    return (jnp.cos(turns).astype(jnp.bfloat16), jnp.sin(turns).astype(jnp.bfloat16))


def centred(spot_px):
    index = jnp.arange(spot_px, dtype=jnp.int32)
    return ((index + spot_px // 2) % spot_px - spot_px // 2).astype(jnp.float32) / spot_px


def along_pixels(values, table):
    return jnp.einsum("iaubv,nv->iaubn", values, table, preferred_element_type=jnp.float32)


def along_rows(table, values):
    return jnp.einsum("mu,iaubn->iabmn", table, values, preferred_element_type=jnp.float32)


def spot_slopes(residual):
    item_count, row_px, col_px = residual.shape
    sub_rows = row_px // SUBPX
    sub_cols = col_px // SUBPX
    cos_t, sin_t = tables(SPOT, SUBPX)
    pieces = residual.reshape(item_count, sub_rows, SUBPX, sub_cols, SUBPX)
    real_part = jnp.cos(pieces).astype(jnp.bfloat16)
    imag_part = jnp.sin(pieces).astype(jnp.bfloat16)
    g_re = (along_pixels(real_part, cos_t) + along_pixels(imag_part, sin_t)).astype(jnp.bfloat16)
    g_im = (along_pixels(imag_part, cos_t) - along_pixels(real_part, sin_t)).astype(jnp.bfloat16)
    h_re = along_rows(cos_t, g_re) + along_rows(sin_t, g_im)
    h_im = along_rows(cos_t, g_im) - along_rows(sin_t, g_re)
    spots = h_re * h_re + h_im * h_im
    coords = centred(SPOT)
    totals = jnp.sum(spots, axis=(3, 4))
    slope_x = jnp.sum(spots * coords[None, None, None, None, :], axis=(3, 4)) / totals
    slope_y = jnp.sum(spots * coords[None, None, None, :, None], axis=(3, 4)) / totals
    return jnp.stack([slope_x, slope_y], axis=-1).reshape(item_count, sub_rows * sub_cols * 2)


def pack_tiles(screens, owners, slots, pairs, my_tile, capacity):
    packed = []
    places = jnp.arange(capacity, dtype=jnp.int32)
    for frame, layer_idx in pairs:
        owner_rows = owners[frame, layer_idx]
        slot_rows = slots[frame, layer_idx]
        mine = owner_rows == my_tile
        order = jnp.cumsum(mine.astype(jnp.int32), axis=1) - 1
        picked = mine[:, None, :] & (order[:, None, :] == places[None, :, None])
        wanted = jnp.sum(jnp.where(picked, slot_rows[:, None, :], 0), axis=2)
        packed.append(jnp.take(screens[layer_idx], wanted, axis=0))
    return jnp.stack(packed, axis=1)


def unpack_tiles(received, owners, pairs, my_tile, capacity):
    results = []
    item_count = owners.shape[3]
    later = jnp.arange(item_count, dtype=jnp.int32)
    earlier_mask = later[None, :] < later[:, None]
    for position in range(len(pairs)):
        frame, layer_idx = pairs[position]
        mine = lax.dynamic_index_in_dim(owners[frame, layer_idx], my_tile, 0, keepdims=False)
        same_owner = mine[:, None] == mine[None, :]
        order = jnp.sum((same_owner & earlier_mask).astype(jnp.int32), axis=1)
        flat_index = mine * capacity + order
        layer_tiles = received[:, position].reshape(-1, received.shape[3], received.shape[4])
        results.append(jnp.take(layer_tiles, flat_index, axis=0).astype(jnp.float32))
    return results


def add_layers(pieces, first_index):
    phase = pieces[first_index]
    phase = phase + pieces[first_index + 1]
    return phase


def per_device(screens, tile_owner, tile_slot, commands_init, reconstructor, pattern):
    layer_total, tiles_here, slab_rows, tile_px = screens.shape
    frame_total = tile_owner.shape[0]
    tile_count = lax.axis_size("tile")
    rec_count = lax.axis_size("rec")
    my_tile = lax.axis_index("tile")
    my_rec = lax.axis_index("rec")
    item_count = LG_DEV + SC_DEV
    capacity = max(2, 3 * item_count // (2 * tile_count))
    owners = tile_owner[..., 0].reshape(frame_total, layer_total, tile_count, item_count)
    slots = tile_slot.reshape(frame_total, layer_total, tile_count, item_count)
    influence_all = influence(tile_px, SUBPX, SUB)
    influence_rows = lax.dynamic_slice_in_dim(influence_all, my_rec * slab_rows, slab_rows, 0)
    lgs_places = (my_tile * LG_DEV + jnp.arange(LG_DEV, dtype=jnp.int32)) % PT
    sci_places = (my_tile * SC_DEV + jnp.arange(SC_DEV, dtype=jnp.int32)) % PT
    item_places = jnp.concatenate([lgs_places, sci_places])
    state = commands_init
    slope_frames = []
    science_frames = []
    for frame in range(frame_total):
        pairs = [(frame, layer_idx) for layer_idx in range(layer_total)]
        sending = pack_tiles(screens, owners, slots, pairs, my_tile, capacity)
        received = lax.all_to_all(sending, "tile", split_axis=0, concat_axis=0, tiled=True)
        pieces = unpack_tiles(received, owners, pairs, my_tile, capacity)
        phase = add_layers(pieces, 0)
        full_commands = lax.all_gather(state, "rec", axis=0, tiled=True)
        mirror = full_commands.reshape(PT, SUB, SUB)
        chosen = jnp.take(mirror, item_places, axis=0)
        shapes = jnp.einsum(
            "xa,iab,yb->ixy", influence_rows, chosen, influence_all, precision=lax.Precision.HIGHEST
        )
        residual = phase - shapes
        science_frames.append(residual[LG_DEV:].astype(jnp.bfloat16))
        slopes = spot_slopes(residual[:LG_DEV])
        slope_frames.append(slopes)
        slopes_b = slopes.astype(jnp.bfloat16)
        everyone = lax.all_gather(slopes_b[None], ("tile", "rec"), axis=0, tiled=True)
        everyone = everyone.reshape(tile_count, rec_count, LG_DEV, -1).transpose(0, 2, 1, 3)
        everyone = everyone.reshape(tile_count * LG_DEV, -1)
        needed = jnp.take(everyone, pattern, axis=0)
        partial_rows = jnp.einsum(
            "ibcs,ibs->ic", reconstructor, needed, preferred_element_type=jnp.float32
        ).reshape(-1)
        state = state + loop_gain * lax.psum(partial_rows, "tile")
    return (jnp.stack(slope_frames, axis=0), jnp.stack(science_frames, axis=0), state)


def solution(mesh):
    placed = (
        P(None, "tile", "rec", None),
        P(),
        P(),
        P("rec"),
        P("rec", "tile", None, None),
        P("rec", "tile"),
    )
    return jax.shard_map(
        per_device,
        mesh=mesh,
        in_specs=placed,
        out_specs=(P(None, "tile", "rec"), P(None, "tile", "rec", None), P("rec")),
        check_vma=False,
    )
```

profile of v0, /device:TPU:0, one launch (start us, length us, event | category | flops | bytes accessed | tf_op | source)
XLA Modules:
  0.0 293.3 jit_solution(11876869289070020217)
XLA Ops:
  3.2 1.2 slice_bitcast_fusion.1
  5.4 1.4 select_bitcast_fusion.2
  9.2 2.0 pad_maximum_fusion
  11.2 7.3 %all-to-all-start = ((bf16[8,2,24,32,128]{4,3,2,1,0:T(8,128)(2,1)}), bf16[8,2,24,32,128]{4,3,2,1,0:T(8,128)(2,1)}, u32[]{:S(2)}, u32[]{:S(2)}) async-start(bf16[8,2,24,32,128]{4,3,2,1,0:T(8,128)(2,1)} %pad_maximum_fusion), calls=%async_computation | async-start | bytes 6291456 | tf_op jit(solution)/shard_map/all_to_all | solution.py:120
  20.5 2.0 gather_fusion.5
  22.5 5.2 %all_gather.12 = f32[4096]{0:T(1024)S(1)} all-gather(f32[1024]{0:T(1024)S(1)} %copy-done.6), channel_id=1, replica_groups=mesh['tile'=8,'rec'=4] {'rec'}, dimensions={0}, use_global_device_ids=true | all-gather | bytes 20480 | tf_op jit(solution)/shard_map/all_gather | solution.py:123
  31.3 2.0 pad_maximum_fusion.1
  33.5 55.7 %all-to-all-done = bf16[8,2,24,32,128]{4,3,2,1,0:T(8,128)(2,1)} async-done(((bf16[8,2,24,32,128]{4,3,2,1,0:T(8,128)(2,1)}), bf16[8,2,24,32,128]{4,3,2,1,0:T(8,128)(2,1)}, u32[]{:S(2)}, u32[]{:S(2)}) %all-to-all-start) | async-done | bytes 3145760 | tf_op jit(solution)/shard_map/all_to_all | solution.py:120
  89.3 4.7 %all-to-all-start.1 = ((bf16[8,2,24,32,128]{4,3,2,1,0:T(8,128)(2,1)}), bf16[8,2,24,32,128]{4,3,2,1,0:T(8,128)(2,1)}, u32[]{:S(2)}, u32[]{:S(2)}) async-start(bf16[8,2,24,32,128]{4,3,2,1,0:T(8,128)(2,1)} %pad_maximum_fusion.1), calls=%async_computation.1 | async-start | bytes 6291456 | tf_op jit(solution)/shard_map/all_to_all | solution.py:120
  94.9 3.7 %fusion.164 = (bf16[8,1,24,32,128]{4,3,2,1,0:T(8,128)(2,1)S(1)}, bf16[8,1,24,32,128]{4,3,2,1,0:T(8,128)(2,1)}) fusion(bf16[8,2,24,32,128]{4,3,2,1,0:T(8,128)(2,1)} %all-to-all-done), kind=kLoop, calls=%fused_computation.284 | loop fusion | bytes 6291456 | tf_op jit(solution)/shard_map/slice | solution.py:87
  98.6 2.2 gather_fusion.3
  100.8 1.7 gather_fusion.2
  102.5 5.7 %add_subtract_fusion.1 = f32[128,32,128]{2,0,1:T(8,128)S(1)} fusion(bf16[128,32,128]{2,1,0:T(8,128)(2,1)S(1)} %gather_fusion.3, bf16[128,32,128]{2,1,0:T(8,128)(2,1)} %gather_fusion.2, pred[128]{0:T(512)(128)(4,1)S(1)} %get-tuple-element.29, pred[128]{0:T(512)(128)(4,1)S(1)} %get-tuple-element.73, f32[128,8,32]{0,2,1:T(8,128)S(1)} %fusion.54, ...), kind=kOutput, calls=%fused_computation.18 | convolution fusion | flops 53482496 | bytes 4326176 | tf_op jit(solution)/shard_map/xa,iab,yb->ixy/dot_general | solution.py:126
  113.4 65.8 %all_gather.13 = bf16[32,4,32]{2,1,0:T(4,128)(2,1)S(1)} all-gather(bf16[1,4,32]{2,1,0:T(4,128)(2,1)S(1)} %copy.90), channel_id=1, replica_groups=mesh['tile'=8,'rec'=4] {'tile','rec'}, dimensions={0}, use_global_device_ids=true | all-gather | bytes 8448 | tf_op jit(solution)/shard_map/all_gather | solution.py:134
  180.3 26.0 %psum.14 = f32[1024]{0:T(1024)S(1)} all-reduce(f32[1024]{0:T(1024)S(1)} %bitcast.175), channel_id=1, replica_groups=mesh['tile'=8,'rec'=4] {'tile'}, use_global_device_ids=true, to_apply=%region_15.20 | all-reduce | flops 1024 | bytes 8192 | tf_op jit(solution)/shard_map/psum | solution.py:141
  206.3 5.4 %all_gather.14 = f32[4096]{0:T(1024)S(1)} all-gather(f32[1024]{0:T(1024)S(1)} %multiply_add_fusion.1), channel_id=1, replica_groups=mesh['tile'=8,'rec'=4] {'rec'}, dimensions={0}, use_global_device_ids=true | all-gather | bytes 20480 | tf_op jit(solution)/shard_map/all_gather | solution.py:123
  213.5 3.7 %fusion.165 = (bf16[8,1,24,32,128]{4,3,2,1,0:T(8,128)(2,1)S(1)}, bf16[8,1,24,32,128]{4,3,2,1,0:T(8,128)(2,1)}) fusion(bf16[8,2,24,32,128]{4,3,2,1,0:T(8,128)(2,1)} %all-to-all-done.1), kind=kLoop, calls=%fused_computation.285 | loop fusion | bytes 6291456 | tf_op jit(solution)/shard_map/slice | solution.py:87
  217.2 2.2 gather_fusion.8
  219.4 1.7 gather_fusion.7
  221.0 5.7 %add_subtract_fusion = f32[128,32,128]{2,0,1:T(8,128)S(1)} fusion(bf16[128,32,128]{2,1,0:T(8,128)(2,1)S(1)} %gather_fusion.8, bf16[128,32,128]{2,1,0:T(8,128)(2,1)} %gather_fusion.7, pred[128]{0:T(512)(128)(4,1)S(1)} %get-tuple-element.37, pred[128]{0:T(512)(128)(4,1)S(1)} %get-tuple-element.71, f32[128,8,32]{0,2,1:T(8,128)S(1)} %fusion.52, ...), kind=kOutput, calls=%fused_computation.17 | convolution fusion | flops 53482496 | bytes 4326176 | tf_op jit(solution)/shard_map/xa,iab,yb->ixy/dot_general | solution.py:126
  230.3 1.3 fusion.11
  234.4 2.6 copy.106
  237.1 36.8 %all_gather.15 = bf16[32,4,32]{2,1,0:T(4,128)(2,1)S(1)} all-gather(bf16[1,4,32]{2,1,0:T(4,128)(2,1)S(1)} %copy.103), channel_id=1, replica_groups=mesh['tile'=8,'rec'=4] {'tile','rec'}, dimensions={0}, use_global_device_ids=true | all-gather | bytes 8448 | tf_op jit(solution)/shard_map/all_gather | solution.py:134
  275.0 17.1 %psum.15 = f32[1024]{0:T(1024)S(1)} all-reduce(f32[1024]{0:T(1024)S(1)} %bitcast.176), channel_id=1, replica_groups=mesh['tile'=8,'rec'=4] {'tile'}, use_global_device_ids=true, to_apply=%region_19.24 | all-reduce | flops 1024 | bytes 8192 | tf_op jit(solution)/shard_map/psum | solution.py:141
  (140 shorter events, 29.0 us)
Async XLA Ops:
  0.6 179.4 %copy-start = (bf16[8,2,128,128]{3,2,1,0:T(8,128)(2,1)S(1)}, bf16[8,2,128,128]{3,2,1,0:T(8,128)(2,1)}, u32[]{:S(2)}) copy-start(bf16[8,2,128,128]{3,2,1,0:T(8,128)(2,1)} %param.18) | copy-start | bytes 1572868
  7.8 1.4 copy-start.2
  11.2 78.1 %all-to-all-start = ((bf16[8,2,24,32,128]{4,3,2,1,0:T(8,128)(2,1)}), bf16[8,2,24,32,128]{4,3,2,1,0:T(8,128)(2,1)}, u32[]{:S(2)}, u32[]{:S(2)}) async-start(bf16[8,2,24,32,128]{4,3,2,1,0:T(8,128)(2,1)} %pad_maximum_fusion), calls=%async_computation | async-start | bytes 6291456 | tf_op jit(solution)/shard_map/all_to_all | solution.py:120
  20.5 2.0 copy-start.6
  20.5 8.3 %copy-start.5 = (s32[2,2,1024,1]{2,3,1,0:T(1,128)S(1)}, s32[2,2,1024,1]{2,3,1,0:T(1,128)}, u32[]{:S(2)}) copy-start(s32[2,2,1024,1]{2,3,1,0:T(1,128)} %param.15) | copy-start | bytes 49156
  29.6 1.4 copy-start.1
  31.3 2.0 copy-start.7
  89.3 124.2 %all-to-all-start.1 = ((bf16[8,2,24,32,128]{4,3,2,1,0:T(8,128)(2,1)}), bf16[8,2,24,32,128]{4,3,2,1,0:T(8,128)(2,1)}, u32[]{:S(2)}, u32[]{:S(2)}) async-start(bf16[8,2,24,32,128]{4,3,2,1,0:T(8,128)(2,1)} %pad_maximum_fusion.1), calls=%async_computation.1 | async-start | bytes 6291456 | tf_op jit(solution)/shard_map/all_to_all | solution.py:120
  108.1 1.4 copy-start.3
  226.7 1.6 copy-start.4
where the time goes:
time: 294 us; the launch traced here: 293 us
  blocking collectives  156 us (53%)
  waiting for transfers between devices  55.7 us (19%)
  local copies, waits for them, and re-layouts  34.4 us (12%)
  matrix products  20.7 us (7%)
  other arithmetic  12.8 us (4%)
  starting transfers between devices  11.9 us (4%)
    all_gather x2, blocking collectives, per_device(): lax.all_gather(slopes_b[None], ('tile', 'rec'), axis=0, tiled=True)  103 us
    all_to_all x2, waiting for transfers between devices, per_device(): lax.all_to_all(sending, 'tile', split_axis=0, concat_axis=0, tiled=True)  55.7 us
    psum x2, blocking collectives, per_device(): state = state + loop_gain * lax.psum(partial_rows, 'tile')  43.2 us
    dot_general x4, matrix products, per_device(): jnp.einsum('xa,iab,yb->ixy', influence_rows, chosen, influence_all, preci...  12.2 us
    all_to_all x2, starting transfers between devices, per_device(): lax.all_to_all(sending, 'tile', split_axis=0, concat_axis=0, tiled=True)  11.9 us
    all_gather x2, blocking collectives, per_device(): full_commands = lax.all_gather(state, 'rec', axis=0, tiled=True)  10.6 us
    gather x4, local copies, waits for them, and re-layouts, unpack_tiles(): jnp.take(layer_tiles, flat_index, axis=0).astype(jnp.float32)  7.65 us
    slice x2, local copies, waits for them, and re-layouts, unpack_tiles(): received[:, position].reshape(-1, received.shape[3], received.shape[4])  7.41 us
  transfers between devices with their start and end apart: 2, of which 1 were waited for; matrix products, arithmetic and copies ran while one was open for 10% of the time, Pallas kernels for 0%

commit v1 on v0

--- a/solution.py
+++ b/solution.py
@@ -138,7 +138,7 @@
         partial_rows = jnp.einsum(
             "ibcs,ibs->ic", reconstructor, needed, preferred_element_type=jnp.float32
         ).reshape(-1)
-        state = state + loop_gain * lax.psum(partial_rows, "tile")
+        state = state + loop_gain * jnp.sum(lax.all_gather(partial_rows, "tile"), axis=0)
     return (jnp.stack(slope_frames, axis=0), jnp.stack(science_frames, axis=0), state)
 
 

time: 294 us -> 320 us (1.088)
  blocking collectives: 156 us -> 182 us
    all_gather x0 -> x2, blocking collectives: none -> 67.4 us  [per_device(): lax.all_gather(partial_rows, 'tile')]
    psum x2 -> x0, blocking collectives: 43.2 us -> none  [per_device(): state = state + loop_gain * lax.psum(partial_rows, 'tile')]
  transfers between devices with their start and end apart: 2 -> 2, of which waited for: 1 -> 1; matrix products, arithmetic and copies ran while one was open for 10% -> 9% of each run, Pallas kernels for 0% -> 0%
where the time goes in v1:
time: 320 us; the launch traced here: 319 us
  blocking collectives  182 us (57%)
  waiting for transfers between devices  55.9 us (17%)
  local copies, waits for them, and re-layouts  34.4 us (11%)
  matrix products  20.7 us (6%)
  other arithmetic  12.8 us (4%)
  starting transfers between devices  11.9 us (4%)
    all_gather x2, blocking collectives, per_device(): lax.all_gather(slopes_b[None], ('tile', 'rec'), axis=0, tiled=True)  104 us
    all_gather x2, blocking collectives, per_device(): lax.all_gather(partial_rows, 'tile')  67.4 us
    all_to_all x2, waiting for transfers between devices, per_device(): lax.all_to_all(sending, 'tile', split_axis=0, concat_axis=0, tiled=True)  55.9 us
    dot_general x4, matrix products, per_device(): jnp.einsum('xa,iab,yb->ixy', influence_rows, chosen, influence_all, preci...  12.2 us
    all_to_all x2, starting transfers between devices, per_device(): lax.all_to_all(sending, 'tile', split_axis=0, concat_axis=0, tiled=True)  11.9 us
    all_gather x2, blocking collectives, per_device(): full_commands = lax.all_gather(state, 'rec', axis=0, tiled=True)  10.6 us
    gather x4, local copies, waits for them, and re-layouts, unpack_tiles(): jnp.take(layer_tiles, flat_index, axis=0).astype(jnp.float32)  7.65 us
    slice x2, local copies, waits for them, and re-layouts, unpack_tiles(): received[:, position].reshape(-1, received.shape[3], received.shape[4])  7.41 us
  transfers between devices with their start and end apart: 2, of which 1 were waited for; matrix products, arithmetic and copies ran while one was open for 9% of the time, Pallas kernels for 0%

profile of v1, /device:TPU:0, one launch (start us, length us, event | category | flops | bytes accessed | tf_op | source)
XLA Modules:
  0.0 319.4 jit_solution(1998445765890395899)
XLA Ops:
  3.2 1.2 slice_bitcast_fusion.1
  5.4 1.4 select_bitcast_fusion.2
  9.2 2.0 pad_maximum_fusion
  11.2 7.3 %all-to-all-start = ((bf16[8,2,24,32,128]{4,3,2,1,0:T(8,128)(2,1)}), bf16[8,2,24,32,128]{4,3,2,1,0:T(8,128)(2,1)}, u32[]{:S(2)}, u32[]{:S(2)}) async-start(bf16[8,2,24,32,128]{4,3,2,1,0:T(8,128)(2,1)} %pad_maximum_fusion), calls=%async_computation | async-start | bytes 6291456 | tf_op jit(solution)/shard_map/all_to_all | solution.py:120
  20.5 2.0 gather_fusion.5
  22.5 5.2 %all_gather.18 = f32[4096]{0:T(1024)S(1)} all-gather(f32[1024]{0:T(1024)S(1)} %copy-done.6), channel_id=1, replica_groups=mesh['tile'=8,'rec'=4] {'rec'}, dimensions={0}, use_global_device_ids=true | all-gather | bytes 20480 | tf_op jit(solution)/shard_map/all_gather | solution.py:123
  31.1 2.0 pad_maximum_fusion.1
  33.3 55.9 %all-to-all-done = bf16[8,2,24,32,128]{4,3,2,1,0:T(8,128)(2,1)} async-done(((bf16[8,2,24,32,128]{4,3,2,1,0:T(8,128)(2,1)}), bf16[8,2,24,32,128]{4,3,2,1,0:T(8,128)(2,1)}, u32[]{:S(2)}, u32[]{:S(2)}) %all-to-all-start) | async-done | bytes 3145760 | tf_op jit(solution)/shard_map/all_to_all | solution.py:120
  89.3 4.7 %all-to-all-start.1 = ((bf16[8,2,24,32,128]{4,3,2,1,0:T(8,128)(2,1)}), bf16[8,2,24,32,128]{4,3,2,1,0:T(8,128)(2,1)}, u32[]{:S(2)}, u32[]{:S(2)}) async-start(bf16[8,2,24,32,128]{4,3,2,1,0:T(8,128)(2,1)} %pad_maximum_fusion.1), calls=%async_computation.1 | async-start | bytes 6291456 | tf_op jit(solution)/shard_map/all_to_all | solution.py:120
  95.1 3.7 %fusion.162 = (bf16[8,1,24,32,128]{4,3,2,1,0:T(8,128)(2,1)S(1)}, bf16[8,1,24,32,128]{4,3,2,1,0:T(8,128)(2,1)}) fusion(bf16[8,2,24,32,128]{4,3,2,1,0:T(8,128)(2,1)} %all-to-all-done), kind=kLoop, calls=%fused_computation.284 | loop fusion | bytes 6291456 | tf_op jit(solution)/shard_map/slice | solution.py:87
  98.8 2.2 gather_fusion.3
  101.0 1.7 gather_fusion.2
  102.6 5.7 %add_subtract_fusion.1 = f32[128,32,128]{2,0,1:T(8,128)S(1)} fusion(bf16[128,32,128]{2,1,0:T(8,128)(2,1)S(1)} %gather_fusion.3, bf16[128,32,128]{2,1,0:T(8,128)(2,1)} %gather_fusion.2, pred[128]{0:T(512)(128)(4,1)S(1)} %get-tuple-element.29, pred[128]{0:T(512)(128)(4,1)S(1)} %get-tuple-element.73, f32[128,8,32]{0,2,1:T(8,128)S(1)} %fusion.52, ...), kind=kOutput, calls=%fused_computation.18 | convolution fusion | flops 53482496 | bytes 4326176 | tf_op jit(solution)/shard_map/xa,iab,yb->ixy/dot_general | solution.py:126
  113.6 65.7 %all_gather.19 = bf16[32,4,32]{2,1,0:T(4,128)(2,1)S(1)} all-gather(bf16[1,4,32]{2,1,0:T(4,128)(2,1)S(1)} %copy.90), channel_id=1, replica_groups=mesh['tile'=8,'rec'=4] {'tile','rec'}, dimensions={0}, use_global_device_ids=true | all-gather | bytes 8448 | tf_op jit(solution)/shard_map/all_gather | solution.py:134
  180.3 36.9 %all-gather = f32[8,1,1024]{2,1,0:T(1,128)S(1)} all-gather(f32[1,1,1024]{2,1,0:T(1,128)S(1)} %convolution_bitcast_fusion.1), channel_id=1, replica_groups=mesh['tile'=8,'rec'=4] {'tile'}, dimensions={0}, use_global_device_ids=true | all-gather | bytes 36864 | tf_op jit(solution)/shard_map/all_gather | solution.py:141
  217.3 5.4 %all_gather.21 = f32[4096]{0:T(1024)S(1)} all-gather(f32[1024]{0:T(1024)S(1)} %multiply_add_fusion.1), channel_id=1, replica_groups=mesh['tile'=8,'rec'=4] {'rec'}, dimensions={0}, use_global_device_ids=true | all-gather | bytes 20480 | tf_op jit(solution)/shard_map/all_gather | solution.py:123
  224.4 3.7 %fusion.163 = (bf16[8,1,24,32,128]{4,3,2,1,0:T(8,128)(2,1)S(1)}, bf16[8,1,24,32,128]{4,3,2,1,0:T(8,128)(2,1)}) fusion(bf16[8,2,24,32,128]{4,3,2,1,0:T(8,128)(2,1)} %all-to-all-done.1), kind=kLoop, calls=%fused_computation.285 | loop fusion | bytes 6291456 | tf_op jit(solution)/shard_map/slice | solution.py:87
  228.1 2.2 gather_fusion.8
  230.3 1.7 gather_fusion.7
  232.0 5.7 %add_subtract_fusion = f32[128,32,128]{2,0,1:T(8,128)S(1)} fusion(bf16[128,32,128]{2,1,0:T(8,128)(2,1)S(1)} %gather_fusion.8, bf16[128,32,128]{2,1,0:T(8,128)(2,1)} %gather_fusion.7, pred[128]{0:T(512)(128)(4,1)S(1)} %get-tuple-element.37, pred[128]{0:T(512)(128)(4,1)S(1)} %get-tuple-element.71, f32[128,8,32]{0,2,1:T(8,128)S(1)} %fusion.50, ...), kind=kOutput, calls=%fused_computation.17 | convolution fusion | flops 53482496 | bytes 4326176 | tf_op jit(solution)/shard_map/xa,iab,yb->ixy/dot_general | solution.py:126
  241.3 1.3 fusion.11
  245.4 2.6 copy.106
  248.1 38.6 %all_gather.22 = bf16[32,4,32]{2,1,0:T(4,128)(2,1)S(1)} all-gather(bf16[1,4,32]{2,1,0:T(4,128)(2,1)S(1)} %copy.103), channel_id=1, replica_groups=mesh['tile'=8,'rec'=4] {'tile','rec'}, dimensions={0}, use_global_device_ids=true | all-gather | bytes 8448 | tf_op jit(solution)/shard_map/all_gather | solution.py:134
  287.7 30.4 %all-gather.1 = f32[8,1,1024]{2,1,0:T(1,128)S(1)} all-gather(f32[1,1,1024]{2,1,0:T(1,128)S(1)} %convolution_bitcast_fusion), channel_id=1, replica_groups=mesh['tile'=8,'rec'=4] {'tile'}, dimensions={0}, use_global_device_ids=true | all-gather | bytes 36864 | tf_op jit(solution)/shard_map/all_gather | solution.py:141
  (142 shorter events, 29.1 us)
Async XLA Ops:
  0.6 179.4 %copy-start = (bf16[8,2,128,128]{3,2,1,0:T(8,128)(2,1)S(1)}, bf16[8,2,128,128]{3,2,1,0:T(8,128)(2,1)}, u32[]{:S(2)}) copy-start(bf16[8,2,128,128]{3,2,1,0:T(8,128)(2,1)} %param.18) | copy-start | bytes 1572868
  7.8 1.4 copy-start.2
  11.2 78.1 %all-to-all-start = ((bf16[8,2,24,32,128]{4,3,2,1,0:T(8,128)(2,1)}), bf16[8,2,24,32,128]{4,3,2,1,0:T(8,128)(2,1)}, u32[]{:S(2)}, u32[]{:S(2)}) async-start(bf16[8,2,24,32,128]{4,3,2,1,0:T(8,128)(2,1)} %pad_maximum_fusion), calls=%async_computation | async-start | bytes 6291456 | tf_op jit(solution)/shard_map/all_to_all | solution.py:120
  20.5 2.0 copy-start.6
  20.5 8.3 %copy-start.5 = (s32[2,2,1024,1]{2,3,1,0:T(1,128)S(1)}, s32[2,2,1024,1]{2,3,1,0:T(1,128)}, u32[]{:S(2)}) copy-start(s32[2,2,1024,1]{2,3,1,0:T(1,128)} %param.15) | copy-start | bytes 49156
  29.4 1.4 copy-start.1
  31.1 2.0 copy-start.7
  89.3 135.2 %all-to-all-start.1 = ((bf16[8,2,24,32,128]{4,3,2,1,0:T(8,128)(2,1)}), bf16[8,2,24,32,128]{4,3,2,1,0:T(8,128)(2,1)}, u32[]{:S(2)}, u32[]{:S(2)}) async-start(bf16[8,2,24,32,128]{4,3,2,1,0:T(8,128)(2,1)} %pad_maximum_fusion.1), calls=%async_computation.1 | async-start | bytes 6291456 | tf_op jit(solution)/shard_map/all_to_all | solution.py:120
  108.3 1.4 copy-start.3
  237.7 1.6 copy-start.4
